TPU v7x, 256 devices: a whole 4x4x8 slice. The times are simulated.
256 devices in a mesh: view: 8 (over x, core), slab: 32 (over y, z).
Axes of the slice: x: 4, y: 4, z: 8, core: 2. Of those that a mesh axis runs over, the one named last changes fastest.
Arguments:
- image: float32 [128, 512, 512], P('slab'), may hold values from 0.1 to 10
- sensitivity: float32 [128, 512, 512], P('slab', 'view'), may hold values from 0.5 to 4
- resample_x: bfloat16 [16, 512, 512], P('view'), may hold values from 0 to 1, as said below
- resample_y: bfloat16 [16, 512, 512], P('view'), may hold values from 0 to 1, as said below
- tof_kernel: bfloat16 [16, 16, 512], P('view'), may hold values from 0.00019454956 to 0.0078125
- axial_mix: float32 [16, 128, 128], P('view'), may hold values from 0 to 1
- background: float32 [16, 16, 512, 128], P('view', None, 'slab'), may hold values from 0.5 to 2
- counts: int32 [16, 16, 512, 128], P('view', None, 'slab'), may hold values from 0 to 19
Outputs:
- new_image: float32 [128, 512, 512], P('slab', 'view')
Inputs may be any that keep to these rules, and one draw needn't show every extreme that they name: resample_x[v, a, x] is zero where |x - a| > 3. resample_y[v, y, b] is zero where |b - y| > 3.
All inputs are finite; a program needn't handle non-finite values.
Results may differ from a plain program's by a relative error of at most 0.00052.
Values may be sent and summed in bfloat16 or wider, within the bound.
A program may use at most 64 MiB of HBM per device.

v0:
```python
import jax
import jax.numpy as jnp
from jax import lax
from jax.sharding import PartitionSpec as P


def local(image, sensitivity, resample_x, resample_y, tof_kernel, axial_mix, background, counts):
    highest = lax.Precision.HIGHEST
    image_low = image.astype(jnp.bfloat16)
    along_y = jnp.einsum(
        "zxy,vyb->vzxb", image_low, resample_y, preferred_element_type=jnp.float32
    ).astype(jnp.bfloat16)
    rotated = jnp.einsum(
        "vzxb,vax->vzba", along_y, resample_x, preferred_element_type=jnp.float32
    ).astype(jnp.bfloat16)
    gathered = lax.all_to_all(rotated, "slab", split_axis=2, concat_axis=1, tiled=True)
    integrals = jnp.einsum(
        "vka,vzba->vkbz", tof_kernel, gathered, preferred_element_type=jnp.float32
    )
    expected = background + jnp.einsum("vkbz,vcz->vkbc", integrals, axial_mix, precision=highest)
    ratios = counts.astype(jnp.float32) / expected
    back_mixed = jnp.einsum("vkbc,vcz->vkbz", ratios, axial_mix, precision=highest).astype(
        jnp.bfloat16
    )
    spread = jnp.einsum(
        "vka,vkbz->vzba", tof_kernel, back_mixed, preferred_element_type=jnp.float32
    ).astype(jnp.bfloat16)
    frames = lax.all_to_all(spread, "slab", split_axis=1, concat_axis=2, tiled=True)
    unrotated = jnp.einsum(
        "vzba,vyb->vzya", frames, resample_y, preferred_element_type=jnp.float32
    ).astype(jnp.bfloat16)
    own_rows = image.shape[1] // lax.axis_size("view")
    gradient = lax.psum_scatter(
        jnp.einsum("vzya,vax->xzy", unrotated, resample_x, preferred_element_type=jnp.float32),
        "view",
        scatter_dimension=0,
        tiled=True,
    )
    gradient = jnp.transpose(gradient, (1, 0, 2))
    current = lax.dynamic_slice_in_dim(image, lax.axis_index("view") * own_rows, own_rows, 1)
    return current * gradient / sensitivity


def solution(mesh):
    in_specs = (
        P("slab", None, None),
        P("slab", "view", None),
        P("view", None, None),
        P("view", None, None),
        P("view", None, None),
        P("view", None, None),
        P("view", None, "slab", None),
        P("view", None, "slab", None),
    )
    out_specs = P("slab", "view", None)
    return jax.shard_map(local, mesh=mesh, in_specs=in_specs, out_specs=out_specs, check_vma=False)
```

profile of v0, /device:TPU:8, one launch (start us, length us, event | category | flops | bytes accessed | tf_op | source)
XLA Modules:
  0.0 340.9 jit_solution(16715669214694171133)
XLA Ops:
  6.5 0.0 copy-start
  6.5 0.0 all-reduce.3.cloned.1.call-start
  6.5 1.2 copy-done
  7.8 8.0 %fusion.8 = bf16[2,4,512,512]{3,2,1,0:T(8,128)(2,1)} fusion(f32[4,512,512]{2,1,0:T(8,128)} %param.8, bf16[2,512,512]{2,1,0:T(8,128)(2,1)S(1)} %copy-done, bf16[2,512,512]{2,1,0:T(8,128)(2,1)} %param.10), kind=kOutput, calls=%fused_computation.9 | convolution fusion | flops 4300210176 | bytes 10485760 | tf_op jit(solution)/shard_map/vzxb,vax->vzba/dot_general | solution.py:13
  15.7 5.4 %copy.44 = bf16[2,4,512,512]{3,1,0,2:T(4,128)(2,1)S(1)} copy(bf16[2,4,512,512]{3,2,1,0:T(8,128)(2,1)} %fusion.8) | data formatting | bytes 8388608 | tf_op jit(solution)/shard_map/convert_element_type | solution.py:15
  21.1 105.1 %all_to_all.36 = bf16[2,4,512,512]{3,1,0,2:T(4,128)(2,1)S(1)} all-to-all(bf16[2,4,512,512]{3,1,0,2:T(4,128)(2,1)S(1)} %copy.44), channel_id=1, replica_groups=mesh['view'=8,'slab'=32] {'slab'}, dimensions={2} | all-to-all | bytes 8388608 | tf_op jit(solution)/shard_map/all_to_all | solution.py:16
  126.2 1.4 copy.45
  127.6 0.0 copy-start.3
  127.6 0.6 copy.46
  128.3 0.1 copy-done.3
  128.4 0.0 copy-start.2
  128.4 1.2 convolution_bitcast_fusion
  129.6 0.8 copy.47
  130.5 0.0 copy-done.2
  130.5 1.4 fusion.24
  131.9 0.4 convolution_convert_fusion
  132.4 2.0 convert_bitcast_fusion
  134.4 2.4 copy.49
  136.8 100.6 %all_to_all.37 = bf16[2,128,16,512]{3,2,0,1:T(8,128)(2,1)S(1)} all-to-all(bf16[2,128,16,512]{3,2,0,1:T(8,128)(2,1)S(1)} %copy.49), channel_id=1, replica_groups=mesh['view'=8,'slab'=32] {'slab'}, dimensions={1} | all-to-all | bytes 8388608 | tf_op jit(solution)/shard_map/all_to_all | solution.py:28
  237.4 0.0 copy-start.4
  237.4 2.4 copy.51
  239.9 0.0 copy-done.4
  239.9 9.2 %fusion.13 = f32[512,4,512]{0,2,1:T(8,128)} fusion(bf16[2,4,512,512]{3,2,1,0:T(8,128)(2,1)} %bitcast.73, bf16[2,512,512]{2,1,0:T(8,128)(2,1)S(1)} %copy-done.4, bf16[2,512,512]{2,1,0:T(8,128)(2,1)S(1)} %copy-done), kind=kOutput, calls=%fused_computation.11 | convolution fusion | flops 4297064448 | bytes 10485760 | tf_op jit(solution)/shard_map/vzya,vax->xzy/dot_general | solution.py:34
  249.1 5.5 %copy.54 = f32[512,4,512]{2,1,0:T(4,128)} copy(f32[512,4,512]{0,2,1:T(8,128)} %fusion.13) | data formatting | bytes 8388608 | tf_op jit(solution)/shard_map/vzya,vax->xzy/dot_general | solution.py:34
  254.5 0.0 copy-start.5
  254.6 0.0 copy-start.1
  254.6 0.0 all-reduce.3.cloned.1.call-update
  254.6 0.6 copy-done.5
  255.2 0.6 dynamic-slice
  256.5 74.4 %all-reduce.3.cloned.1.call-done = f32[512,4,512]{2,1,0:T(4,128)} async-done(((f32[512,4,512]{2,1,0:T(4,128)}), f32[512,4,512]{2,1,0:T(4,128)}) %all-reduce.3.cloned.1.call-update) | async-done | bytes 4194320
  330.9 1.1 constant_dynamic-slice_fusion
  331.9 0.0 copy-done.1
  332.0 2.1 fusion.31
Async XLA Ops:
  6.5 1.2 copy-start
  6.5 324.3 %all-reduce.3.cloned.1.call-start = ((), (), s32[]{:S(2)}) async-start(), calls=%async_computation.2 | async-start | bytes 8388608
  127.6 0.8 copy-start.3
  128.4 2.1 copy-start.2
  237.4 2.5 copy-start.4
  254.5 0.7 copy-start.5
  254.6 77.4 %copy-start.1 = (f32[4,64,512]{2,1,0:T(8,128)S(1)}, f32[4,64,512]{2,1,0:T(8,128)}, u32[]{:S(2)}) copy-start(f32[4,64,512]{2,1,0:T(8,128)} %param.9) | copy-start | bytes 1572868
Sparse Core Ops, SparseCore 0:
  254.7 76.1 all-reduce.2
where the time goes:
time: 341 us
  blocking collectives  206 us (60%)
  waiting for transfers between devices  74.4 us (22%)
  local copies, waits for them, and re-layouts  22.3 us (7%)
  matrix products  22.3 us (7%)
  between operations  14.1 us (4%)
    all_to_all x1, blocking collectives, local(): lax.all_to_all(rotated, 'slab', split_axis=2, concat_axis=1, tiled=True)  105 us
    all_to_all x1, blocking collectives, local(): lax.all_to_all(spread, 'slab', split_axis=1, concat_axis=2, tiled=True)  101 us
    unnamed x2, waiting for transfers between devices  74.4 us
    dot_general x1, matrix products, local(): jnp.einsum('vzya,vax->xzy', unrotated, resample_x, preferred_element_type...  9.19 us
    dot_general x1, matrix products, local(): jnp.einsum('vzxb,vax->vzba', along_y, resample_x, preferred_element_type=...  7.96 us
  transfers between devices with their start and end apart: 1, of which 1 were waited for; matrix products, arithmetic and copies ran while one was open for 0% of the time, Pallas kernels for 0%

commit v1 on v0

--- a/solution.py
+++ b/solution.py
@@ -13,7 +13,12 @@
     rotated = jnp.einsum(
         "vzxb,vax->vzba", along_y, resample_x, preferred_element_type=jnp.float32
     ).astype(jnp.bfloat16)
-    gathered = lax.all_to_all(rotated, "slab", split_axis=2, concat_axis=1, tiled=True)
+    gathered = jnp.concatenate(
+        jax.lax.all_to_all(
+            jnp.stack(jnp.split(rotated, jax.lax.axis_size("slab"), axis=2)), "slab", 0, 0
+        ),
+        axis=1,
+    )
     integrals = jnp.einsum(
         "vka,vzba->vkbz", tof_kernel, gathered, preferred_element_type=jnp.float32
     )

time: 341 us -> 365 us (1.070)
  local copies, waits for them, and re-layouts: 22.3 us -> 44.9 us
    unnamed x14 -> x45, local copies, waits for them, and re-layouts: 3.64 us -> 32.1 us
    convert_element_type x1 -> x0, local copies, waits for them, and re-layouts: 5.42 us -> none  [local(): rotated = jnp.einsum('vzxb,vax->vzba', along_y, resample_x, preferred_ele...]
where the time goes in v1:
time: 365 us; the launch traced here: 364 us
  blocking collectives  206 us (56%)
  waiting for transfers between devices  74.6 us (20%)
  local copies, waits for them, and re-layouts  44.9 us (12%)
  matrix products  22.3 us (6%)
  between operations  14.2 us (4%)
    all_to_all x1, blocking collectives, local(): jax.lax.all_to_all(jnp.stack(jnp.split(rotated, jax.lax.axis_size('slab')...  105 us
    all_to_all x1, blocking collectives, local(): lax.all_to_all(spread, 'slab', split_axis=1, concat_axis=2, tiled=True)  101 us
    unnamed x2, waiting for transfers between devices  74.6 us
    unnamed x45, local copies, waits for them, and re-layouts  32.1 us
    dot_general x1, matrix products, local(): jnp.einsum('vzya,vax->xzy', unrotated, resample_x, preferred_element_type...  9.19 us
    dot_general x1, matrix products, local(): jnp.einsum('vzxb,vax->vzba', along_y, resample_x, preferred_element_type=...  7.96 us
  transfers between devices with their start and end apart: 1, of which 1 were waited for; matrix products, arithmetic and copies ran while one was open for 0% of the time, Pallas kernels for 0%

profile of v1, /device:TPU:8, one launch (start us, length us, event | category | flops | bytes accessed | tf_op | source)
XLA Modules:
  0.0 363.8 jit_solution(4648365904659545570)
XLA Ops:
  6.5 0.0 copy-start
  6.5 0.0 all-reduce.3.cloned.1.call-start
  6.5 1.2 copy-done
  7.8 8.0 %fusion.8 = bf16[2,4,512,512]{3,2,1,0:T(8,128)(2,1)} fusion(f32[4,512,512]{2,1,0:T(8,128)} %param.8, bf16[2,512,512]{2,1,0:T(8,128)(2,1)S(1)} %copy-done, bf16[2,512,512]{2,1,0:T(8,128)(2,1)} %param.10), kind=kOutput, calls=%fused_computation.9 | convolution fusion | flops 4300210176 | bytes 10485760 | tf_op jit(solution)/shard_map/vzxb,vax->vzba/dot_general | solution.py:13
  15.7 0.9 fusion.64
  16.6 0.9 fusion.63
  17.6 0.9 fusion.62
  18.5 0.9 fusion.61
  19.4 0.9 fusion.60
  20.3 0.9 fusion.59
  21.3 0.9 fusion.58
  22.2 0.9 fusion.57
  23.1 0.9 fusion.56
  24.0 0.9 fusion.55
  24.9 0.9 fusion.54
  25.9 0.9 fusion.53
  26.8 0.9 fusion.52
  27.7 0.9 fusion.51
  28.6 0.9 fusion.50
  29.6 0.9 fusion.49
  30.5 0.9 fusion.48
  31.4 0.9 fusion.47
  32.3 0.9 fusion.46
  33.3 0.9 fusion.45
  34.2 0.9 fusion.44
  35.1 0.9 fusion.43
  36.0 0.9 fusion.42
  36.9 0.9 fusion.41
  37.9 0.9 fusion.40
  38.8 0.9 fusion.39
  39.7 0.9 fusion.38
  40.6 0.9 fusion.37
  41.6 0.9 fusion.36
  42.5 0.9 fusion.35
  43.4 0.9 fusion.34
  44.3 0.9 fusion.33
  45.3 105.0 %all_to_all.23 = bf16[32,2,4,16,512]{4,3,2,1,0:T(8,128)(2,1)S(1)} all-to-all(bf16[32,2,4,16,512]{4,3,2,1,0:T(8,128)(2,1)S(1)} %fusion.33), channel_id=1, replica_groups=mesh['view'=8,'slab'=32] {'slab'}, dimensions={0} | all-to-all | bytes 8388608 | tf_op jit(solution)/shard_map/all_to_all | solution.py:17
  150.2 0.0 copy-start.3
  150.2 0.8 copy.42
  151.1 0.0 copy-done.3
  151.1 0.0 copy-start.2
  151.1 1.2 convolution_bitcast_fusion
  152.3 0.8 copy.43
  153.1 0.0 copy-done.2
  153.1 1.4 fusion.24
  154.6 0.4 convolution_convert_fusion
  155.0 2.0 convert_bitcast_fusion
  157.1 2.4 copy.45
  159.5 100.6 %all_to_all.24 = bf16[2,128,16,512]{3,2,0,1:T(8,128)(2,1)S(1)} all-to-all(bf16[2,128,16,512]{3,2,0,1:T(8,128)(2,1)S(1)} %copy.45), channel_id=1, replica_groups=mesh['view'=8,'slab'=32] {'slab'}, dimensions={1} | all-to-all | bytes 8388608 | tf_op jit(solution)/shard_map/all_to_all | solution.py:33
  260.1 0.0 copy-start.4
  260.1 2.4 copy.47
  262.6 0.0 copy-done.4
  262.6 9.2 %fusion.13 = f32[512,4,512]{0,2,1:T(8,128)} fusion(bf16[2,4,512,512]{3,2,1,0:T(8,128)(2,1)} %bitcast.199, bf16[2,512,512]{2,1,0:T(8,128)(2,1)S(1)} %copy-done.4, bf16[2,512,512]{2,1,0:T(8,128)(2,1)S(1)} %copy-done), kind=kOutput, calls=%fused_computation.11 | convolution fusion | flops 4297064448 | bytes 10485760 | tf_op jit(solution)/shard_map/vzya,vax->xzy/dot_general | solution.py:39
  271.8 5.5 %copy.50 = f32[512,4,512]{2,1,0:T(4,128)} copy(f32[512,4,512]{0,2,1:T(8,128)} %fusion.13) | data formatting | bytes 8388608 | tf_op jit(solution)/shard_map/vzya,vax->xzy/dot_general | solution.py:39
  277.2 0.0 copy-start.5
  277.2 0.0 copy-start.1
  277.2 0.0 all-reduce.3.cloned.1.call-update
  277.3 0.6 copy-done.5
  277.9 0.6 dynamic-slice
  279.2 74.6 %all-reduce.3.cloned.1.call-done = f32[512,4,512]{2,1,0:T(4,128)} async-done(((f32[512,4,512]{2,1,0:T(4,128)}), f32[512,4,512]{2,1,0:T(4,128)}) %all-reduce.3.cloned.1.call-update) | async-done | bytes 4194320
  353.7 1.1 constant_dynamic-slice_fusion
  354.8 0.0 copy-done.1
  354.8 2.1 fusion.31
Async XLA Ops:
  6.5 1.2 copy-start
  6.5 347.2 %all-reduce.3.cloned.1.call-start = ((), (), s32[]{:S(2)}) async-start(), calls=%async_computation.2 | async-start | bytes 8388608
  150.2 0.8 copy-start.3
  151.1 2.1 copy-start.2
  260.1 2.5 copy-start.4
  277.2 0.7 copy-start.5
  277.2 77.6 %copy-start.1 = (f32[4,64,512]{2,1,0:T(8,128)S(1)}, f32[4,64,512]{2,1,0:T(8,128)}, u32[]{:S(2)}) copy-start(f32[4,64,512]{2,1,0:T(8,128)} %param.9) | copy-start | bytes 1572868
Sparse Core Ops, SparseCore 0:
  277.4 76.2 all-reduce.2
